TPU v7x, 128 devices: a whole 4x4x4 slice. The times are simulated.
128 devices in a mesh: stripe: 32 (over x, y_lo, z), sub: 4 (over y_hi, core).
Axes of the slice: x: 4, y: 4 (y_hi: 2, y_lo: 2; y = y_hi * 2 + y_lo), z: 4, core: 2. Of those that a mesh axis runs over, the one named last changes fastest.
Arguments:
- channel: float32 [8, 32, 64, 512], P('sub', 'stripe'), may hold values from -0.25 to 0.25
- received: float32 [8, 32, 2048], P('sub', None, 'stripe'), may hold values from -18 to 18
- noise_var: float32 [8, 32], P('sub', 'stripe'), may hold values from 0.25 to 4
- downlink: float32 [8, 32, 512], P('sub'), may hold values from -6 to 6
- user_order: int32 [512], P('stripe'), may hold values from 0 to 511, each once
Outputs:
- transmit: float32 [8, 32, 2048], P('sub', None, 'stripe')
- owned: float32 [8, 32, 512], P('sub', None, 'stripe')
Inputs may be any that keep to these rules, and one draw needn't show every extreme that they name: `user_order`: a permutation of the 512 users.
All inputs are finite; a program needn't handle non-finite values.
Results may differ from a plain program's by a relative error of at most 0.00017.
Values sent between devices are 32-bit elements; how exact they have to be, the bound alone decides.
No kernel may reach another device: no remote copies, remote signals or barrier semaphores. Data moves between devices by JAX's collectives and lax.ppermute only.
A program may use at most 256 MiB of HBM per device.

v0:
```python
import jax
import jax.numpy as jnp
from jax import lax
from jax.sharding import PartitionSpec as P

prior_var = 0.1


def from_behind(value, axis, steps):
    count = lax.axis_size(axis)
    first, last = (max(0, -steps), min(count, count - steps))
    return lax.ppermute(value, axis, [(source, source + steps) for source in range(first, last)])


def from_root(block, axis, source):
    block = jnp.where(lax.axis_index(axis) == source, block, jnp.zeros_like(block))
    return lax.psum(block, axis)


def product(left, right):
    return jnp.dot(left, right, precision=lax.Precision.HIGHEST, preferred_element_type=jnp.float32)


def woodbury(covariance, estimate, matrix, samples, variance):
    cross_term = product(covariance, matrix.T)
    system = product(matrix, cross_term) + variance * jnp.eye(matrix.shape[0], dtype=jnp.float32)
    factor = jnp.linalg.cholesky(system)
    gain_rows = jax.scipy.linalg.cho_solve((factor, True), cross_term.T)
    residual_rows = samples - product(estimate, matrix.T)
    estimate = estimate + product(residual_rows, gain_rows)
    covariance = covariance - product(cross_term, gain_rows)
    return (covariance, estimate)


def shards(channel, received, noise_var, downlink, user_order):
    local_blocks, local_links, antennas, user_count = channel.shape
    symbols = received.shape[1]
    samples = received.reshape(local_blocks, symbols, local_links, antennas).transpose(0, 2, 1, 3)
    eye_users = jnp.eye(user_count, dtype=jnp.float32)
    position = lax.axis_index("stripe")
    length = lax.axis_size("stripe")
    prior_cov = prior_var * eye_users
    prior_est = jnp.zeros((symbols, user_count), jnp.float32)

    def apply_links(covariance, estimate, block_index):
        matrices = lax.dynamic_index_in_dim(channel, block_index, 0, keepdims=False)
        sample_rows = lax.dynamic_index_in_dim(samples, block_index, 0, keepdims=False)
        variances = lax.dynamic_index_in_dim(noise_var, block_index, 0, keepdims=False)
        covariance, estimate = woodbury(
            covariance, estimate, matrices[0], sample_rows[0], variances[0]
        )
        return (covariance, estimate)

    def one_turn(turn_index, carried):
        out_cov, out_est, kept_cov, kept_est = carried
        in_cov, in_est = from_behind((out_cov, out_est), "stripe", 1)
        is_first = position == 0
        in_cov = jnp.where(is_first, prior_cov, in_cov)
        in_est = jnp.where(is_first, prior_est, in_est)
        block_index = turn_index - position
        is_valid = (block_index >= 0) & (block_index < local_blocks)
        clipped = jnp.clip(block_index, 0, local_blocks - 1)
        new_cov, new_est = apply_links(in_cov, in_est, clipped)
        keep_it = is_valid & (position == length - 1)
        old_cov = lax.dynamic_index_in_dim(kept_cov, clipped, 0, keepdims=False)
        old_est = lax.dynamic_index_in_dim(kept_est, clipped, 0, keepdims=False)
        kept_cov = lax.dynamic_update_index_in_dim(
            kept_cov, jnp.where(keep_it, new_cov, old_cov), clipped, 0
        )
        kept_est = lax.dynamic_update_index_in_dim(
            kept_est, jnp.where(keep_it, new_est, old_est), clipped, 0
        )
        return (new_cov, new_est, kept_cov, kept_est)

    initial = (
        prior_cov,
        prior_est,
        jnp.zeros((local_blocks, user_count, user_count), jnp.float32),
        jnp.zeros((local_blocks, symbols, user_count), jnp.float32),
    )
    carried = lax.fori_loop(0, local_blocks + length - 1, one_turn, initial)
    covars, estimates = (
        from_root(carried[2], "stripe", length - 1),
        from_root(carried[3], "stripe", length - 1),
    )
    diag_sum = jnp.sum(jnp.diagonal(covars, axis1=1, axis2=2), axis=0)
    total = lax.psum(diag_sum, "sub")
    mean_error = total / (local_blocks * lax.axis_size("sub"))
    power_scale = lax.rsqrt(mean_error)
    precoded = (
        jnp.einsum("bsk,bkn->bsn", downlink, covars, precision=lax.Precision.HIGHEST) * power_scale
    )
    transmit = jnp.einsum("bsk,blmk->bslm", precoded, channel, precision=lax.Precision.HIGHEST)
    transmit = transmit.reshape(local_blocks, symbols, local_links * antennas)
    owned_rows = jnp.take(estimates, user_order, axis=2)
    return (transmit, owned_rows)


def solution(mesh):
    return jax.shard_map(
        shards,
        mesh=mesh,
        in_specs=(
            P("sub", "stripe", None, None),
            P("sub", None, "stripe"),
            P("sub", "stripe"),
            P("sub", None, None),
            P("stripe"),
        ),
        out_specs=(P("sub", None, "stripe"), P("sub", None, "stripe")),
        check_vma=False,
    )
```

profile of v0, /device:TPU:1, one launch (start us, length us, event | category | flops | bytes accessed | tf_op | source)
XLA Modules:
  0.0 1959.1 jit_solution(15671876080877473592)
XLA Ops:
  9.3 1484.5 %while.21 = (s32[]{:T(128)}, f32[512,512]{1,0:T(8,128)}, f32[32,512]{1,0:T(8,128)S(1)}, f32[2,512,512]{2,1,0:T(8,128)S(1)}, f32[2,32,512]{2,1,0:T(8,128)}, /*ind...) while((s32[]{:T(128)}, f32[512,512]{1,0:T(8,128)}, ...), condition=%wide.region_3.4_spmd.clone, body=%wide.region_0.3_spmd.clone.sunk | while | flops 505559104 | bytes 14437732 | solution.py:81
  20.0 17.1 collective-permute-done.1
  42.8 6.6 cholesky.65
  59.2 6.8 collective-permute-start
  71.3 16.3 collective-permute-done.1
  93.3 6.6 cholesky.65
  109.7 6.8 collective-permute-start
  121.8 15.6 collective-permute-done.1
  143.1 6.6 cholesky.65
  159.5 6.8 collective-permute-start
  171.6 14.8 collective-permute-done.1
  192.1 6.6 cholesky.65
  208.5 6.8 collective-permute-start
  221.8 12.9 collective-permute-done.1
  240.4 6.6 cholesky.65
  256.8 7.1 collective-permute-start
  272.3 10.1 collective-permute-done.1
  288.0 6.6 cholesky.65
  304.4 9.2 collective-permute-start
  322.0 9.3 collective-permute-done.1
  337.0 6.6 cholesky.65
  353.4 9.2 collective-permute-start
  370.9 8.5 collective-permute-done.1
  401.6 9.3 collective-permute-start
  419.1 7.9 collective-permute-done.1
  449.1 9.1 collective-permute-start
  466.6 7.0 collective-permute-done.1
  495.7 9.3 collective-permute-start
  541.7 9.3 collective-permute-start
  587.0 9.3 collective-permute-start
  631.6 9.2 collective-permute-start
  658.9 6.6 cholesky.65
  675.3 9.3 collective-permute-start
  701.8 6.6 cholesky.65
  718.2 9.1 collective-permute-start
  761.0 9.3 collective-permute-start
  787.6 6.6 cholesky.65
  804.0 9.0 collective-permute-start
  830.3 6.6 cholesky.65
  846.7 8.9 collective-permute-start
  889.4 8.8 collective-permute-start
  915.5 6.6 cholesky.65
  931.9 10.1 collective-permute-start
  975.6 9.9 collective-permute-start
  1002.9 6.6 cholesky.65
  1019.2 9.8 collective-permute-start
  1046.3 6.6 cholesky.65
  1062.7 9.4 collective-permute-start
  1105.8 9.4 collective-permute-start
  1148.9 9.4 collective-permute-start
  1175.7 6.6 cholesky.65
  1192.0 9.4 collective-permute-start
  1235.1 9.4 collective-permute-start
  1261.9 6.6 cholesky.65
  1278.3 9.4 collective-permute-start
  1321.4 9.4 collective-permute-start
  1348.1 6.6 cholesky.65
  1364.5 9.4 collective-permute-start
  1407.6 9.4 collective-permute-start
  1450.7 9.4 collective-permute-start
  1477.4 6.6 cholesky.65
  1496.7 355.5 %all-reduce.3.cloned.1.call-done = (f32[2,512,512]{2,1,0:T(8,128)}, f32[2,32,512]{2,1,0:T(8,128)}) async-done(((f32[2,512,512]{2,1,0:T(8,128)}, f32[2,32,512]{2,1,0:T(8,128)}), (f32[2,512,512]{2,1,0:T(8,128)}, f32[2,32,512]{2,1,0:T(8,128)})) %all-reduce.3.cloned.1.call-update) | async-done | bytes 2228240 | tf_op jit(solution)/shard_map/psum | solution.py:17
  1854.7 60.2 %copy.23 = f32[2,512,512]{0,2,1:T(8,128)} copy(f32[2,512,512]{2,1,0:T(8,128)} %get-tuple-element.308) | data formatting | bytes 4194304 | tf_op jit(solution)/shard_map/psum | solution.py:17
  1920.6 28.3 %psum.22 = f32[512]{0:T(512)S(1)} all-reduce(f32[512]{0:T(512)S(1)} %reduce_sum.9), channel_id=1, replica_groups=mesh['stripe'=32,'sub'=4] {'sub'}, use_global_device_ids=true, to_apply=%region_6.7 | all-reduce | flops 512 | bytes 4096 | tf_op jit(solution)/shard_map/psum | solution.py:87
  (759 shorter events, 972.4 us)
Async XLA Ops:
  7.2 1845.1 %all-reduce.3.cloned.1.call-start = ((), (), s32[]{:S(2)}) async-start(), calls=%async_computation | async-start | bytes 4456448 | tf_op jit(solution)/shard_map/psum | solution.py:17
  9.3 29.0 %collective-permute-start = (f32[512,512]{1,0:T(8,128)}, f32[512,512]{1,0:T(8,128)}, u32[]{:S(2)}, u32[]{:S(2)}) collective-permute-start(f32[512,512]{1,0:T(8,128)} %get-tuple-element.404), channel_id=1, source_target_pairs={{0,4},{4,8},{8,12},{12,16},{16,20},{20,24},{24,28},{28,32},{32,36}... | collective-permute-start | bytes 3145736 | tf_op jit(solution)/shard_map/while/body/eval_jaxpr/ppermute | solution.py:12
  14.7 22.4 %collective-permute-start.1 = (f32[32,512]{1,0:T(8,128)S(1)}, f32[32,512]{1,0:T(8,128)S(1)}, u32[]{:S(2)}, u32[]{:S(2)}) collective-permute-start(f32[32,512]{1,0:T(8,128)S(1)} %broadcast_select_fusion.4), channel_id=1, source_target_pairs={{0,4},{4,8},{8,12},{12,16},{16,20},{20,24},{24,28},{28,32},{32,36}... | collective-permute-start | bytes 196616 | tf_op jit(solution)/shard_map/while/body/eval_jaxpr/ppermute | solution.py:12
  59.2 29.6 %collective-permute-start = (f32[512,512]{1,0:T(8,128)}, f32[512,512]{1,0:T(8,128)}, u32[]{:S(2)}, u32[]{:S(2)}) collective-permute-start(f32[512,512]{1,0:T(8,128)} %get-tuple-element.404), channel_id=1, source_target_pairs={{0,4},{4,8},{8,12},{12,16},{16,20},{20,24},{24,28},{28,32},{32,36}... | collective-permute-start | bytes 3145736 | tf_op jit(solution)/shard_map/while/body/eval_jaxpr/ppermute | solution.py:12
  66.0 21.6 %collective-permute-start.1 = (f32[32,512]{1,0:T(8,128)S(1)}, f32[32,512]{1,0:T(8,128)S(1)}, u32[]{:S(2)}, u32[]{:S(2)}) collective-permute-start(f32[32,512]{1,0:T(8,128)S(1)} %broadcast_select_fusion.4), channel_id=1, source_target_pairs={{0,4},{4,8},{8,12},{12,16},{16,20},{20,24},{24,28},{28,32},{32,36}... | collective-permute-start | bytes 196616 | tf_op jit(solution)/shard_map/while/body/eval_jaxpr/ppermute | solution.py:12
  109.7 28.8 %collective-permute-start = (f32[512,512]{1,0:T(8,128)}, f32[512,512]{1,0:T(8,128)}, u32[]{:S(2)}, u32[]{:S(2)}) collective-permute-start(f32[512,512]{1,0:T(8,128)} %get-tuple-element.404), channel_id=1, source_target_pairs={{0,4},{4,8},{8,12},{12,16},{16,20},{20,24},{24,28},{28,32},{32,36}... | collective-permute-start | bytes 3145736 | tf_op jit(solution)/shard_map/while/body/eval_jaxpr/ppermute | solution.py:12
  116.5 20.9 %collective-permute-start.1 = (f32[32,512]{1,0:T(8,128)S(1)}, f32[32,512]{1,0:T(8,128)S(1)}, u32[]{:S(2)}, u32[]{:S(2)}) collective-permute-start(f32[32,512]{1,0:T(8,128)S(1)} %broadcast_select_fusion.4), channel_id=1, source_target_pairs={{0,4},{4,8},{8,12},{12,16},{16,20},{20,24},{24,28},{28,32},{32,36}... | collective-permute-start | bytes 196616 | tf_op jit(solution)/shard_map/while/body/eval_jaxpr/ppermute | solution.py:12
  159.5 28.1 %collective-permute-start = (f32[512,512]{1,0:T(8,128)}, f32[512,512]{1,0:T(8,128)}, u32[]{:S(2)}, u32[]{:S(2)}) collective-permute-start(f32[512,512]{1,0:T(8,128)} %get-tuple-element.404), channel_id=1, source_target_pairs={{0,4},{4,8},{8,12},{12,16},{16,20},{20,24},{24,28},{28,32},{32,36}... | collective-permute-start | bytes 3145736 | tf_op jit(solution)/shard_map/while/body/eval_jaxpr/ppermute | solution.py:12
  166.3 20.1 %collective-permute-start.1 = (f32[32,512]{1,0:T(8,128)S(1)}, f32[32,512]{1,0:T(8,128)S(1)}, u32[]{:S(2)}, u32[]{:S(2)}) collective-permute-start(f32[32,512]{1,0:T(8,128)S(1)} %broadcast_select_fusion.4), channel_id=1, source_target_pairs={{0,4},{4,8},{8,12},{12,16},{16,20},{20,24},{24,28},{28,32},{32,36}... | collective-permute-start | bytes 196616 | tf_op jit(solution)/shard_map/while/body/eval_jaxpr/ppermute | solution.py:12
  208.5 27.4 %collective-permute-start = (f32[512,512]{1,0:T(8,128)}, f32[512,512]{1,0:T(8,128)}, u32[]{:S(2)}, u32[]{:S(2)}) collective-permute-start(f32[512,512]{1,0:T(8,128)} %get-tuple-element.404), channel_id=1, source_target_pairs={{0,4},{4,8},{8,12},{12,16},{16,20},{20,24},{24,28},{28,32},{32,36}... | collective-permute-start | bytes 3145736 | tf_op jit(solution)/shard_map/while/body/eval_jaxpr/ppermute | solution.py:12
  215.4 19.4 collective-permute-start.1
  256.8 26.7 %collective-permute-start = (f32[512,512]{1,0:T(8,128)}, f32[512,512]{1,0:T(8,128)}, u32[]{:S(2)}, u32[]{:S(2)}) collective-permute-start(f32[512,512]{1,0:T(8,128)} %get-tuple-element.404), channel_id=1, source_target_pairs={{0,4},{4,8},{8,12},{12,16},{16,20},{20,24},{24,28},{28,32},{32,36}... | collective-permute-start | bytes 3145736 | tf_op jit(solution)/shard_map/while/body/eval_jaxpr/ppermute | solution.py:12
  264.0 18.4 collective-permute-start.1
  304.4 28.0 %collective-permute-start = (f32[512,512]{1,0:T(8,128)}, f32[512,512]{1,0:T(8,128)}, u32[]{:S(2)}, u32[]{:S(2)}) collective-permute-start(f32[512,512]{1,0:T(8,128)} %get-tuple-element.404), channel_id=1, source_target_pairs={{0,4},{4,8},{8,12},{12,16},{16,20},{20,24},{24,28},{28,32},{32,36}... | collective-permute-start | bytes 3145736 | tf_op jit(solution)/shard_map/while/body/eval_jaxpr/ppermute | solution.py:12
  313.6 17.6 collective-permute-start.1
  353.4 27.3 %collective-permute-start = (f32[512,512]{1,0:T(8,128)}, f32[512,512]{1,0:T(8,128)}, u32[]{:S(2)}, u32[]{:S(2)}) collective-permute-start(f32[512,512]{1,0:T(8,128)} %get-tuple-element.404), channel_id=1, source_target_pairs={{0,4},{4,8},{8,12},{12,16},{16,20},{20,24},{24,28},{28,32},{32,36}... | collective-permute-start | bytes 3145736 | tf_op jit(solution)/shard_map/while/body/eval_jaxpr/ppermute | solution.py:12
  362.6 16.9 collective-permute-start.1
  401.6 26.6 %collective-permute-start = (f32[512,512]{1,0:T(8,128)}, f32[512,512]{1,0:T(8,128)}, u32[]{:S(2)}, u32[]{:S(2)}) collective-permute-start(f32[512,512]{1,0:T(8,128)} %get-tuple-element.404), channel_id=1, source_target_pairs={{0,4},{4,8},{8,12},{12,16},{16,20},{20,24},{24,28},{28,32},{32,36}... | collective-permute-start | bytes 3145736 | tf_op jit(solution)/shard_map/while/body/eval_jaxpr/ppermute | solution.py:12
  410.8 16.1 collective-permute-start.1
  449.1 25.6 %collective-permute-start = (f32[512,512]{1,0:T(8,128)}, f32[512,512]{1,0:T(8,128)}, u32[]{:S(2)}, u32[]{:S(2)}) collective-permute-start(f32[512,512]{1,0:T(8,128)} %get-tuple-element.404), channel_id=1, source_target_pairs={{0,4},{4,8},{8,12},{12,16},{16,20},{20,24},{24,28},{28,32},{32,36}... | collective-permute-start | bytes 3145736 | tf_op jit(solution)/shard_map/while/body/eval_jaxpr/ppermute | solution.py:12
  458.2 15.4 collective-permute-start.1
  495.7 25.1 %collective-permute-start = (f32[512,512]{1,0:T(8,128)}, f32[512,512]{1,0:T(8,128)}, u32[]{:S(2)}, u32[]{:S(2)}) collective-permute-start(f32[512,512]{1,0:T(8,128)} %get-tuple-element.404), channel_id=1, source_target_pairs={{0,4},{4,8},{8,12},{12,16},{16,20},{20,24},{24,28},{28,32},{32,36}... | collective-permute-start | bytes 3145736 | tf_op jit(solution)/shard_map/while/body/eval_jaxpr/ppermute | solution.py:12
  505.0 14.6 collective-permute-start.1
  541.7 24.4 %collective-permute-start = (f32[512,512]{1,0:T(8,128)}, f32[512,512]{1,0:T(8,128)}, u32[]{:S(2)}, u32[]{:S(2)}) collective-permute-start(f32[512,512]{1,0:T(8,128)} %get-tuple-element.404), channel_id=1, source_target_pairs={{0,4},{4,8},{8,12},{12,16},{16,20},{20,24},{24,28},{28,32},{32,36}... | collective-permute-start | bytes 3145736 | tf_op jit(solution)/shard_map/while/body/eval_jaxpr/ppermute | solution.py:12
  551.0 13.9 collective-permute-start.1
  587.0 23.6 %collective-permute-start = (f32[512,512]{1,0:T(8,128)}, f32[512,512]{1,0:T(8,128)}, u32[]{:S(2)}, u32[]{:S(2)}) collective-permute-start(f32[512,512]{1,0:T(8,128)} %get-tuple-element.404), channel_id=1, source_target_pairs={{0,4},{4,8},{8,12},{12,16},{16,20},{20,24},{24,28},{28,32},{32,36}... | collective-permute-start | bytes 3145736 | tf_op jit(solution)/shard_map/while/body/eval_jaxpr/ppermute | solution.py:12
  596.3 13.2 collective-permute-start.1
  631.6 22.7 %collective-permute-start = (f32[512,512]{1,0:T(8,128)}, f32[512,512]{1,0:T(8,128)}, u32[]{:S(2)}, u32[]{:S(2)}) collective-permute-start(f32[512,512]{1,0:T(8,128)} %get-tuple-element.404), channel_id=1, source_target_pairs={{0,4},{4,8},{8,12},{12,16},{16,20},{20,24},{24,28},{28,32},{32,36}... | collective-permute-start | bytes 3145736 | tf_op jit(solution)/shard_map/while/body/eval_jaxpr/ppermute | solution.py:12
  640.8 12.4 collective-permute-start.1
  675.3 22.0 %collective-permute-start = (f32[512,512]{1,0:T(8,128)}, f32[512,512]{1,0:T(8,128)}, u32[]{:S(2)}, u32[]{:S(2)}) collective-permute-start(f32[512,512]{1,0:T(8,128)} %get-tuple-element.404), channel_id=1, source_target_pairs={{0,4},{4,8},{8,12},{12,16},{16,20},{20,24},{24,28},{28,32},{32,36}... | collective-permute-start | bytes 3145736 | tf_op jit(solution)/shard_map/while/body/eval_jaxpr/ppermute | solution.py:12
  684.5 11.6 collective-permute-start.1
  718.2 21.9 %collective-permute-start = (f32[512,512]{1,0:T(8,128)}, f32[512,512]{1,0:T(8,128)}, u32[]{:S(2)}, u32[]{:S(2)}) collective-permute-start(f32[512,512]{1,0:T(8,128)} %get-tuple-element.404), channel_id=1, source_target_pairs={{0,4},{4,8},{8,12},{12,16},{16,20},{20,24},{24,28},{28,32},{32,36}... | collective-permute-start | bytes 3145736 | tf_op jit(solution)/shard_map/while/body/eval_jaxpr/ppermute | solution.py:12
  727.4 11.6 collective-permute-start.1
  761.0 22.0 %collective-permute-start = (f32[512,512]{1,0:T(8,128)}, f32[512,512]{1,0:T(8,128)}, u32[]{:S(2)}, u32[]{:S(2)}) collective-permute-start(f32[512,512]{1,0:T(8,128)} %get-tuple-element.404), channel_id=1, source_target_pairs={{0,4},{4,8},{8,12},{12,16},{16,20},{20,24},{24,28},{28,32},{32,36}... | collective-permute-start | bytes 3145736 | tf_op jit(solution)/shard_map/while/body/eval_jaxpr/ppermute | solution.py:12
  770.3 11.6 collective-permute-start.1
  804.0 21.8 %collective-permute-start = (f32[512,512]{1,0:T(8,128)}, f32[512,512]{1,0:T(8,128)}, u32[]{:S(2)}, u32[]{:S(2)}) collective-permute-start(f32[512,512]{1,0:T(8,128)} %get-tuple-element.404), channel_id=1, source_target_pairs={{0,4},{4,8},{8,12},{12,16},{16,20},{20,24},{24,28},{28,32},{32,36}... | collective-permute-start | bytes 3145736 | tf_op jit(solution)/shard_map/while/body/eval_jaxpr/ppermute | solution.py:12
  813.0 11.6 collective-permute-start.1
  846.7 21.7 %collective-permute-start = (f32[512,512]{1,0:T(8,128)}, f32[512,512]{1,0:T(8,128)}, u32[]{:S(2)}, u32[]{:S(2)}) collective-permute-start(f32[512,512]{1,0:T(8,128)} %get-tuple-element.404), channel_id=1, source_target_pairs={{0,4},{4,8},{8,12},{12,16},{16,20},{20,24},{24,28},{28,32},{32,36}... | collective-permute-start | bytes 3145736 | tf_op jit(solution)/shard_map/while/body/eval_jaxpr/ppermute | solution.py:12
  855.7 11.6 collective-permute-start.1
  889.4 21.6 %collective-permute-start = (f32[512,512]{1,0:T(8,128)}, f32[512,512]{1,0:T(8,128)}, u32[]{:S(2)}, u32[]{:S(2)}) collective-permute-start(f32[512,512]{1,0:T(8,128)} %get-tuple-element.404), channel_id=1, source_target_pairs={{0,4},{4,8},{8,12},{12,16},{16,20},{20,24},{24,28},{28,32},{32,36}... | collective-permute-start | bytes 3145736 | tf_op jit(solution)/shard_map/while/body/eval_jaxpr/ppermute | solution.py:12
  898.2 11.6 collective-permute-start.1
  931.9 22.8 %collective-permute-start = (f32[512,512]{1,0:T(8,128)}, f32[512,512]{1,0:T(8,128)}, u32[]{:S(2)}, u32[]{:S(2)}) collective-permute-start(f32[512,512]{1,0:T(8,128)} %get-tuple-element.404), channel_id=1, source_target_pairs={{0,4},{4,8},{8,12},{12,16},{16,20},{20,24},{24,28},{28,32},{32,36}... | collective-permute-start | bytes 3145736 | tf_op jit(solution)/shard_map/while/body/eval_jaxpr/ppermute | solution.py:12
  941.9 11.6 collective-permute-start.1
  975.6 22.7 %collective-permute-start = (f32[512,512]{1,0:T(8,128)}, f32[512,512]{1,0:T(8,128)}, u32[]{:S(2)}, u32[]{:S(2)}) collective-permute-start(f32[512,512]{1,0:T(8,128)} %get-tuple-element.404), channel_id=1, source_target_pairs={{0,4},{4,8},{8,12},{12,16},{16,20},{20,24},{24,28},{28,32},{32,36}... | collective-permute-start | bytes 3145736 | tf_op jit(solution)/shard_map/while/body/eval_jaxpr/ppermute | solution.py:12
  985.6 11.6 collective-permute-start.1
  1019.2 22.5 %collective-permute-start = (f32[512,512]{1,0:T(8,128)}, f32[512,512]{1,0:T(8,128)}, u32[]{:S(2)}, u32[]{:S(2)}) collective-permute-start(f32[512,512]{1,0:T(8,128)} %get-tuple-element.404), channel_id=1, source_target_pairs={{0,4},{4,8},{8,12},{12,16},{16,20},{20,24},{24,28},{28,32},{32,36}... | collective-permute-start | bytes 3145736 | tf_op jit(solution)/shard_map/while/body/eval_jaxpr/ppermute | solution.py:12
  1029.0 11.6 collective-permute-start.1
  1062.7 22.2 %collective-permute-start = (f32[512,512]{1,0:T(8,128)}, f32[512,512]{1,0:T(8,128)}, u32[]{:S(2)}, u32[]{:S(2)}) collective-permute-start(f32[512,512]{1,0:T(8,128)} %get-tuple-element.404), channel_id=1, source_target_pairs={{0,4},{4,8},{8,12},{12,16},{16,20},{20,24},{24,28},{28,32},{32,36}... | collective-permute-start | bytes 3145736 | tf_op jit(solution)/shard_map/while/body/eval_jaxpr/ppermute | solution.py:12
  1072.1 11.6 collective-permute-start.1
  1105.8 22.2 %collective-permute-start = (f32[512,512]{1,0:T(8,128)}, f32[512,512]{1,0:T(8,128)}, u32[]{:S(2)}, u32[]{:S(2)}) collective-permute-start(f32[512,512]{1,0:T(8,128)} %get-tuple-element.404), channel_id=1, source_target_pairs={{0,4},{4,8},{8,12},{12,16},{16,20},{20,24},{24,28},{28,32},{32,36}... | collective-permute-start | bytes 3145736 | tf_op jit(solution)/shard_map/while/body/eval_jaxpr/ppermute | solution.py:12
  1115.2 11.6 collective-permute-start.1
  1148.9 22.2 %collective-permute-start = (f32[512,512]{1,0:T(8,128)}, f32[512,512]{1,0:T(8,128)}, u32[]{:S(2)}, u32[]{:S(2)}) collective-permute-start(f32[512,512]{1,0:T(8,128)} %get-tuple-element.404), channel_id=1, source_target_pairs={{0,4},{4,8},{8,12},{12,16},{16,20},{20,24},{24,28},{28,32},{32,36}... | collective-permute-start | bytes 3145736 | tf_op jit(solution)/shard_map/while/body/eval_jaxpr/ppermute | solution.py:12
  1158.4 11.6 collective-permute-start.1
  1192.0 22.2 %collective-permute-start = (f32[512,512]{1,0:T(8,128)}, f32[512,512]{1,0:T(8,128)}, u32[]{:S(2)}, u32[]{:S(2)}) collective-permute-start(f32[512,512]{1,0:T(8,128)} %get-tuple-element.404), channel_id=1, source_target_pairs={{0,4},{4,8},{8,12},{12,16},{16,20},{20,24},{24,28},{28,32},{32,36}... | collective-permute-start | bytes 3145736 | tf_op jit(solution)/shard_map/while/body/eval_jaxpr/ppermute | solution.py:12
  1201.5 11.6 collective-permute-start.1
  1235.1 22.2 %collective-permute-start = (f32[512,512]{1,0:T(8,128)}, f32[512,512]{1,0:T(8,128)}, u32[]{:S(2)}, u32[]{:S(2)}) collective-permute-start(f32[512,512]{1,0:T(8,128)} %get-tuple-element.404), channel_id=1, source_target_pairs={{0,4},{4,8},{8,12},{12,16},{16,20},{20,24},{24,28},{28,32},{32,36}... | collective-permute-start | bytes 3145736 | tf_op jit(solution)/shard_map/while/body/eval_jaxpr/ppermute | solution.py:12
  1278.3 22.2 %collective-permute-start = (f32[512,512]{1,0:T(8,128)}, f32[512,512]{1,0:T(8,128)}, u32[]{:S(2)}, u32[]{:S(2)}) collective-permute-start(f32[512,512]{1,0:T(8,128)} %get-tuple-element.404), channel_id=1, source_target_pairs={{0,4},{4,8},{8,12},{12,16},{16,20},{20,24},{24,28},{28,32},{32,36}... | collective-permute-start | bytes 3145736 | tf_op jit(solution)/shard_map/while/body/eval_jaxpr/ppermute | solution.py:12
  1287.7 11.6 collective-permute-start.1
  1321.4 22.2 %collective-permute-start = (f32[512,512]{1,0:T(8,128)}, f32[512,512]{1,0:T(8,128)}, u32[]{:S(2)}, u32[]{:S(2)}) collective-permute-start(f32[512,512]{1,0:T(8,128)} %get-tuple-element.404), channel_id=1, source_target_pairs={{0,4},{4,8},{8,12},{12,16},{16,20},{20,24},{24,28},{28,32},{32,36}... | collective-permute-start | bytes 3145736 | tf_op jit(solution)/shard_map/while/body/eval_jaxpr/ppermute | solution.py:12
  1364.5 22.2 %collective-permute-start = (f32[512,512]{1,0:T(8,128)}, f32[512,512]{1,0:T(8,128)}, u32[]{:S(2)}, u32[]{:S(2)}) collective-permute-start(f32[512,512]{1,0:T(8,128)} %get-tuple-element.404), channel_id=1, source_target_pairs={{0,4},{4,8},{8,12},{12,16},{16,20},{20,24},{24,28},{28,32},{32,36}... | collective-permute-start | bytes 3145736 | tf_op jit(solution)/shard_map/while/body/eval_jaxpr/ppermute | solution.py:12
  1373.9 11.6 collective-permute-start.1
  1407.6 22.2 %collective-permute-start = (f32[512,512]{1,0:T(8,128)}, f32[512,512]{1,0:T(8,128)}, u32[]{:S(2)}, u32[]{:S(2)}) collective-permute-start(f32[512,512]{1,0:T(8,128)} %get-tuple-element.404), channel_id=1, source_target_pairs={{0,4},{4,8},{8,12},{12,16},{16,20},{20,24},{24,28},{28,32},{32,36}... | collective-permute-start | bytes 3145736 | tf_op jit(solution)/shard_map/while/body/eval_jaxpr/ppermute | solution.py:12
  1450.7 22.2 %collective-permute-start = (f32[512,512]{1,0:T(8,128)}, f32[512,512]{1,0:T(8,128)}, u32[]{:S(2)}, u32[]{:S(2)}) collective-permute-start(f32[512,512]{1,0:T(8,128)} %get-tuple-element.404), channel_id=1, source_target_pairs={{0,4},{4,8},{8,12},{12,16},{16,20},{20,24},{24,28},{28,32},{32,36}... | collective-permute-start | bytes 3145736 | tf_op jit(solution)/shard_map/while/body/eval_jaxpr/ppermute | solution.py:12
  1460.1 11.6 collective-permute-start.1
  (39 other events, 2141.0 us)
Sparse Core Ops, SparseCore 0:
  1496.2 356.0 all-reduce.2
where the time goes:
time: 1970 us; the launch traced here: 1960 us
  waiting for transfers between devices  553 us (28%)
  other arithmetic  467 us (24%)
  starting transfers between devices  465 us (24%)
  matrix products  264 us (13%)
  local copies, waits for them, and re-layouts  164 us (8%)
  blocking collectives  28.3 us (1%)
    ppermute x66, starting transfers between devices, from_behind(): lax.ppermute(value, axis, [(source, source + steps) for source in range(f...  465 us
    psum x1, waiting for transfers between devices, from_root(): return lax.psum(block, axis)  356 us
    dot_general x165, matrix products, product(): jnp.dot(left, right, precision=lax.Precision.HIGHEST, preferred_element_t...  241 us
    another operation x99, other arithmetic, woodbury(): factor = jnp.linalg.cholesky(system)  240 us
    ppermute x66, waiting for transfers between devices, from_behind(): lax.ppermute(value, axis, [(source, source + steps) for source in range(f...  198 us
    another operation x66, other arithmetic, woodbury(): gain_rows = jax.scipy.linalg.cho_solve((factor, True), cross_term.T)  183 us
    psum x2, local copies, waits for them, and re-layouts, from_root(): return lax.psum(block, axis)  61.3 us
    dynamic_slice x33, local copies, waits for them, and re-layouts, one_turn(): old_est = lax.dynamic_index_in_dim(kept_est, clipped, 0, keepdims=False)  48.5 us
  transfers between devices with their start and end apart: 67, of which 34 were waited for; matrix products, arithmetic and copies ran while one was open for 7% of the time, Pallas kernels for 0%

commit v1 on v0

--- a/solution.py
+++ b/solution.py
@@ -14,7 +14,7 @@
 
 def from_root(block, axis, source):
     block = jnp.where(lax.axis_index(axis) == source, block, jnp.zeros_like(block))
-    return lax.psum(block, axis)
+    return jnp.sum(lax.all_gather(block, axis), axis=0)
 
 
 def product(left, right):

time: 1970 us -> 2550 us (1.29)
  waiting for transfers between devices: 553 us -> 1100 us
  other arithmetic: 467 us -> 518 us
    all_gather x0 -> x2, waiting for transfers between devices: none -> 927 us  [from_root(): return jnp.sum(lax.all_gather(block, axis), axis=0)]
    psum x1 -> x0, waiting for transfers between devices: 356 us -> none  [from_root(): return lax.psum(block, axis)]
    psum x2 -> x0, local copies, waits for them, and re-layouts: 61.3 us -> none  [from_root(): return lax.psum(block, axis)]
    reduce_sum x0 -> x2, local copies, waits for them, and re-layouts: none -> 59.7 us  [from_root(): return jnp.sum(lax.all_gather(block, axis), axis=0)]
    ppermute x66, waiting for transfers between devices: 198 us -> 170 us  [from_behind(): lax.ppermute(value, axis, [(source, source + steps) for source in range(f...]
    while x33, other arithmetic: 0.24 us -> 27.1 us
  transfers between devices with their start and end apart: 67 -> 68, of which waited for: 34 -> 35; matrix products, arithmetic and copies ran while one was open for 7% -> 6% of each run, Pallas kernels for 0% -> 0%
where the time goes in v1:
time: 2550 us; the launch traced here: 2530 us
  waiting for transfers between devices  1100 us (43%)
  other arithmetic  518 us (20%)
  starting transfers between devices  465 us (18%)
  matrix products  265 us (10%)
  local copies, waits for them, and re-layouts  163 us (6%)
    all_gather x2, waiting for transfers between devices, from_root(): return jnp.sum(lax.all_gather(block, axis), axis=0)  927 us
    ppermute x66, starting transfers between devices, from_behind(): lax.ppermute(value, axis, [(source, source + steps) for source in range(f...  465 us
    dot_general x165, matrix products, product(): jnp.dot(left, right, precision=lax.Precision.HIGHEST, preferred_element_t...  242 us
    another operation x99, other arithmetic, woodbury(): factor = jnp.linalg.cholesky(system)  240 us
    another operation x66, other arithmetic, woodbury(): gain_rows = jax.scipy.linalg.cho_solve((factor, True), cross_term.T)  183 us
    ppermute x66, waiting for transfers between devices, from_behind(): lax.ppermute(value, axis, [(source, source + steps) for source in range(f...  170 us
    reduce_sum x2, local copies, waits for them, and re-layouts, from_root(): return jnp.sum(lax.all_gather(block, axis), axis=0)  59.7 us
  transfers between devices with their start and end apart: 68, of which 35 were waited for; matrix products, arithmetic and copies ran while one was open for 6% of the time, Pallas kernels for 0%

profile of v1, /device:TPU:1, one launch (start us, length us, event | category | flops | bytes accessed | tf_op | source)
XLA Modules:
  0.0 2534.0 jit_solution(9312097905576407171)
XLA Ops:
  9.3 1486.9 %while.21 = (s32[]{:T(128)}, f32[512,512]{1,0:T(8,128)}, f32[32,512]{1,0:T(8,128)}, f32[2,512,512]{2,1,0:T(8,128)S(1)}, f32[2,32,512]{2,1,0:T(8,128)}, /*index=5...) while((s32[]{:T(128)}, f32[512,512]{1,0:T(8,128)}, ...), condition=%wide.region_3.4_spmd.clone, body=%wide.region_0.3_spmd.clone.sunk | while | flops 505559104 | bytes 14437732 | solution.py:81
  20.1 17.0 collective-permute-done.1
  42.8 6.6 cholesky.65
  59.2 6.8 collective-permute-start
  72.2 15.5 collective-permute-done.1
  93.5 6.6 cholesky.65
  109.9 6.8 collective-permute-start
  122.9 14.7 collective-permute-done.1
  143.3 6.6 cholesky.65
  159.7 6.8 collective-permute-start
  172.7 14.0 collective-permute-done.1
  192.5 6.6 cholesky.65
  208.9 6.8 collective-permute-start
  223.0 12.1 collective-permute-done.1
  240.8 6.6 cholesky.65
  257.2 7.1 collective-permute-start
  273.6 9.2 collective-permute-done.1
  288.5 6.6 cholesky.65
  304.9 9.3 collective-permute-start
  323.4 8.5 collective-permute-done.1
  337.7 6.6 cholesky.65
  354.1 9.2 collective-permute-start
  372.4 7.7 collective-permute-done.1
  385.9 6.6 cholesky.65
  402.3 9.2 collective-permute-start
  420.7 7.0 collective-permute-done.1
  433.4 6.6 cholesky.65
  449.8 9.3 collective-permute-start
  480.2 6.6 cholesky.65
  496.6 9.2 collective-permute-start
  542.6 9.3 collective-permute-start
  588.0 9.2 collective-permute-start
  616.1 6.6 cholesky.65
  632.5 9.2 collective-permute-start
  659.8 6.6 cholesky.65
  676.3 9.3 collective-permute-start
  719.3 9.1 collective-permute-start
  762.2 9.3 collective-permute-start
  788.8 6.6 cholesky.65
  805.3 9.0 collective-permute-start
  848.0 8.9 collective-permute-start
  890.7 8.9 collective-permute-start
  916.9 6.6 cholesky.65
  933.3 10.0 collective-permute-start
  977.1 9.9 collective-permute-start
  1020.8 9.8 collective-permute-start
  1048.0 6.6 cholesky.65
  1064.4 9.4 collective-permute-start
  1107.6 9.4 collective-permute-start
  1150.7 9.4 collective-permute-start
  1193.9 9.4 collective-permute-start
  1237.1 9.4 collective-permute-start
  1263.9 6.6 cholesky.65
  1280.3 9.4 collective-permute-start
  1307.0 6.6 cholesky.65
  1323.4 9.4 collective-permute-start
  1366.6 9.4 collective-permute-start
  1409.8 9.4 collective-permute-start
  1453.0 9.4 collective-permute-start
  1499.1 196.6 %all-gather.7.cloned.1.call-done = f32[64,32,512]{2,1,0:T(8,128)} async-done(((f32[2,32,512]{2,1,0:T(8,128)}), f32[64,32,512]{2,1,0:T(8,128)}) %all-gather.7.cloned.1.call-update) | async-done | bytes 4194320 | tf_op jit(solution)/shard_map/all_gather | solution.py:17
  1699.9 730.6 %all-gather.5.cloned.1.call-done = f32[64,512,512]{2,1,0:T(8,128)} async-done(((f32[2,512,512]{2,1,0:T(8,128)}), f32[64,512,512]{2,1,0:T(8,128)}) %all-gather.5.cloned.1.call-update) | async-done | bytes 67108880 | tf_op jit(solution)/shard_map/all_gather | solution.py:17
  2430.5 20.9 reduce_sum.27
  2451.4 59.5 %copy.11 = f32[2,512,512]{0,2,1:T(8,128)} copy(f32[2,512,512]{2,1,0:T(8,128)S(1)} %reduce_sum.27) | data formatting | bytes 4194304 | tf_op jit(solution)/shard_map/reduce_sum | solution.py:17
  2516.5 7.4 psum.7
  (762 shorter events, 996.9 us)
Async XLA Ops:
  7.2 1688.6 %all-gather.7.cloned.1.call-start = ((), (), s32[]{:S(2)}) async-start(), calls=%async_computation.1 | async-start | bytes 4325376 | tf_op jit(solution)/shard_map/all_gather | solution.py:17
  9.3 29.0 %collective-permute-start = (f32[512,512]{1,0:T(8,128)}, f32[512,512]{1,0:T(8,128)}, u32[]{:S(2)}, u32[]{:S(2)}) collective-permute-start(f32[512,512]{1,0:T(8,128)} %get-tuple-element.380), channel_id=1, source_target_pairs={{0,4},{4,8},{8,12},{12,16},{16,20},{20,24},{24,28},{28,32},{32,36}... | collective-permute-start | bytes 3145736 | tf_op jit(solution)/shard_map/while/body/eval_jaxpr/ppermute | solution.py:12
  14.7 22.4 collective-permute-start.1
  59.2 29.6 %collective-permute-start = (f32[512,512]{1,0:T(8,128)}, f32[512,512]{1,0:T(8,128)}, u32[]{:S(2)}, u32[]{:S(2)}) collective-permute-start(f32[512,512]{1,0:T(8,128)} %get-tuple-element.380), channel_id=1, source_target_pairs={{0,4},{4,8},{8,12},{12,16},{16,20},{20,24},{24,28},{28,32},{32,36}... | collective-permute-start | bytes 3145736 | tf_op jit(solution)/shard_map/while/body/eval_jaxpr/ppermute | solution.py:12
  66.9 20.8 collective-permute-start.1
  109.9 28.9 %collective-permute-start = (f32[512,512]{1,0:T(8,128)}, f32[512,512]{1,0:T(8,128)}, u32[]{:S(2)}, u32[]{:S(2)}) collective-permute-start(f32[512,512]{1,0:T(8,128)} %get-tuple-element.380), channel_id=1, source_target_pairs={{0,4},{4,8},{8,12},{12,16},{16,20},{20,24},{24,28},{28,32},{32,36}... | collective-permute-start | bytes 3145736 | tf_op jit(solution)/shard_map/while/body/eval_jaxpr/ppermute | solution.py:12
  117.5 20.1 collective-permute-start.1
  159.7 28.1 %collective-permute-start = (f32[512,512]{1,0:T(8,128)}, f32[512,512]{1,0:T(8,128)}, u32[]{:S(2)}, u32[]{:S(2)}) collective-permute-start(f32[512,512]{1,0:T(8,128)} %get-tuple-element.380), channel_id=1, source_target_pairs={{0,4},{4,8},{8,12},{12,16},{16,20},{20,24},{24,28},{28,32},{32,36}... | collective-permute-start | bytes 3145736 | tf_op jit(solution)/shard_map/while/body/eval_jaxpr/ppermute | solution.py:12
  167.4 19.3 collective-permute-start.1
  208.9 27.4 %collective-permute-start = (f32[512,512]{1,0:T(8,128)}, f32[512,512]{1,0:T(8,128)}, u32[]{:S(2)}, u32[]{:S(2)}) collective-permute-start(f32[512,512]{1,0:T(8,128)} %get-tuple-element.380), channel_id=1, source_target_pairs={{0,4},{4,8},{8,12},{12,16},{16,20},{20,24},{24,28},{28,32},{32,36}... | collective-permute-start | bytes 3145736 | tf_op jit(solution)/shard_map/while/body/eval_jaxpr/ppermute | solution.py:12
  216.5 18.6 collective-permute-start.1
  257.2 26.7 %collective-permute-start = (f32[512,512]{1,0:T(8,128)}, f32[512,512]{1,0:T(8,128)}, u32[]{:S(2)}, u32[]{:S(2)}) collective-permute-start(f32[512,512]{1,0:T(8,128)} %get-tuple-element.380), channel_id=1, source_target_pairs={{0,4},{4,8},{8,12},{12,16},{16,20},{20,24},{24,28},{28,32},{32,36}... | collective-permute-start | bytes 3145736 | tf_op jit(solution)/shard_map/while/body/eval_jaxpr/ppermute | solution.py:12
  265.2 17.5 collective-permute-start.1
  304.9 28.1 %collective-permute-start = (f32[512,512]{1,0:T(8,128)}, f32[512,512]{1,0:T(8,128)}, u32[]{:S(2)}, u32[]{:S(2)}) collective-permute-start(f32[512,512]{1,0:T(8,128)} %get-tuple-element.380), channel_id=1, source_target_pairs={{0,4},{4,8},{8,12},{12,16},{16,20},{20,24},{24,28},{28,32},{32,36}... | collective-permute-start | bytes 3145736 | tf_op jit(solution)/shard_map/while/body/eval_jaxpr/ppermute | solution.py:12
  315.1 16.8 collective-permute-start.1
  354.1 27.2 %collective-permute-start = (f32[512,512]{1,0:T(8,128)}, f32[512,512]{1,0:T(8,128)}, u32[]{:S(2)}, u32[]{:S(2)}) collective-permute-start(f32[512,512]{1,0:T(8,128)} %get-tuple-element.380), channel_id=1, source_target_pairs={{0,4},{4,8},{8,12},{12,16},{16,20},{20,24},{24,28},{28,32},{32,36}... | collective-permute-start | bytes 3145736 | tf_op jit(solution)/shard_map/while/body/eval_jaxpr/ppermute | solution.py:12
  364.1 16.1 collective-permute-start.1
  402.3 26.5 %collective-permute-start = (f32[512,512]{1,0:T(8,128)}, f32[512,512]{1,0:T(8,128)}, u32[]{:S(2)}, u32[]{:S(2)}) collective-permute-start(f32[512,512]{1,0:T(8,128)} %get-tuple-element.380), channel_id=1, source_target_pairs={{0,4},{4,8},{8,12},{12,16},{16,20},{20,24},{24,28},{28,32},{32,36}... | collective-permute-start | bytes 3145736 | tf_op jit(solution)/shard_map/while/body/eval_jaxpr/ppermute | solution.py:12
  412.4 15.3 collective-permute-start.1
  449.8 25.8 %collective-permute-start = (f32[512,512]{1,0:T(8,128)}, f32[512,512]{1,0:T(8,128)}, u32[]{:S(2)}, u32[]{:S(2)}) collective-permute-start(f32[512,512]{1,0:T(8,128)} %get-tuple-element.380), channel_id=1, source_target_pairs={{0,4},{4,8},{8,12},{12,16},{16,20},{20,24},{24,28},{28,32},{32,36}... | collective-permute-start | bytes 3145736 | tf_op jit(solution)/shard_map/while/body/eval_jaxpr/ppermute | solution.py:12
  459.9 14.5 collective-permute-start.1
  496.6 25.0 collective-permute-start
  506.7 13.8 collective-permute-start.1
  542.6 24.3 collective-permute-start
  552.8 13.1 collective-permute-start.1
  588.0 23.5 collective-permute-start
  598.0 12.3 collective-permute-start.1
  632.5 22.8 collective-permute-start
  642.6 11.5 collective-permute-start.1
  676.3 22.1 collective-permute-start
  686.4 10.8 collective-permute-start.1
  719.3 21.9 collective-permute-start
  729.3 10.8 collective-permute-start.1
  762.2 22.0 collective-permute-start
  772.3 10.8 collective-permute-start.1
  805.3 21.8 collective-permute-start
  815.1 10.8 collective-permute-start.1
  848.0 21.7 collective-permute-start
  857.8 10.8 collective-permute-start.1
  890.7 21.6 collective-permute-start
  900.4 10.8 collective-permute-start.1
  933.3 22.8 collective-permute-start
  944.2 10.8 collective-permute-start.1
  977.1 22.7 collective-permute-start
  987.9 10.8 collective-permute-start.1
  1020.8 22.6 collective-permute-start
  1031.5 10.8 collective-permute-start.1
  1064.4 22.2 collective-permute-start
  1074.7 10.8 collective-permute-start.1
  1107.6 22.2 collective-permute-start
  1117.8 10.8 collective-permute-start.1
  1150.7 22.2 collective-permute-start
  1161.0 10.8 collective-permute-start.1
  1193.9 22.2 collective-permute-start
  1237.1 22.2 collective-permute-start
  1280.3 22.2 collective-permute-start
  1323.4 22.2 collective-permute-start
  1366.6 22.2 collective-permute-start
  1376.9 10.8 collective-permute-start.1
  1409.8 22.2 collective-permute-start
  1420.1 10.8 collective-permute-start.1
  1453.0 22.2 collective-permute-start
  1463.2 10.8 collective-permute-start.1
  1496.8 933.6 %all-gather.5.cloned.1.call-start = ((), (), s32[]{:S(2)}) async-start(), calls=%async_computation | async-start | bytes 69206016 | tf_op jit(solution)/shard_map/all_gather | solution.py:17
  (39 other events, 2630.1 us)
Sparse Core Ops, SparseCore 0:
  1497.0 198.7 all-gather.6
  1697.4 732.9 all-gather.4
